TPU v7x, 512 devices: a whole 4x4x16 slice. The times are simulated.
512 devices in a mesh: section: 4 (over z_hi), dp: 8 (over x, core), tensor: 16 (over z_lo, y).
Axes of the slice: x: 4, y: 4, z: 16 (z_hi: 4, z_lo: 4; z = z_hi * 4 + z_lo), core: 2. Of those that a mesh axis runs over, the one named last changes fastest.
Arguments:
- hidden: bfloat16 [4, 1024, 28672], P('section', 'tensor', 'dp'), may hold values from -6 to 6
- down_weight: bfloat16 [4, 28672, 8192], P('section', 'dp', 'tensor'), may hold values from -0.03125 to 0.03125
- residual: bfloat16 [4, 1024, 8192], P('section', 'dp', 'tensor'), may hold values from -36 to 36
- norm_gain: float32 [4, 8192], P('section', 'tensor'), may hold values from 0.4 to 1.2
- query_weight: bfloat16 [4, 8192, 4096], P('section', 'tensor', 'dp'), may hold values from -0.0625 to 0.0625
- key_value_weight: bfloat16 [4, 8192, 2048], P('section', 'tensor', 'dp'), may hold values from -0.0625 to 0.0625
Outputs:
- attention: bfloat16 [4, 1024, 4096], P('section', 'tensor', 'dp')
All inputs are finite; a program needn't handle non-finite values.
Results may differ from a plain program's by a relative error of at most 0.04.
Values may be sent and summed in bfloat16 or wider, within the bound.
A program may use at most 64 MiB of HBM per device.

v0:
```python
import jax
import jax.numpy as jnp
from jax import lax
from jax.sharding import PartitionSpec as P

D = 8192
HD = 128
ROPE_BASE = 500000.0
EPSILON = 1e-05


def passed_along(value, axis, steps):
    count = lax.axis_size(axis)
    pairs = [(source, (source + steps) % count) for source in range(count)]
    return lax.ppermute(value, axis, pairs)


def rotate(values, positions):
    half_dim = values.shape[-1] // 2
    frequency = ROPE_BASE ** (-jnp.arange(half_dim, dtype=jnp.float32) * 2.0 / values.shape[-1])
    angles = positions.astype(jnp.float32)[:, None] * frequency[None, :]
    cosine = jnp.cos(angles)[:, None, :]
    sine_part = jnp.sin(angles)[:, None, :]
    front_part = values[..., :half_dim]
    back_part = values[..., half_dim:]
    return jnp.concatenate(
        [front_part * cosine - back_part * sine_part, back_part * cosine + front_part * sine_part],
        axis=-1,
    )


def per_device(hidden, down_weight, residual, norm_gain, query_weight, key_value_weight):
    weight_block = down_weight[0]
    partials = jnp.dot(
        lax.all_gather(hidden[0], "tensor", axis=0, tiled=True),
        weight_block,
        preferred_element_type=jnp.float32,
    )
    summed = lax.psum_scatter(
        partials.astype(jnp.bfloat16), "dp", scatter_dimension=0, tiled=True
    ).astype(jnp.float32)
    boundary = (residual[0].astype(jnp.float32) + summed).astype(jnp.bfloat16)
    gathered = lax.all_gather(boundary, "dp", axis=0, tiled=True)
    arrived = passed_along(gathered, "section", 1)
    values_in = arrived.astype(jnp.float32)
    squares = jnp.sum(values_in * values_in, axis=1)
    scaled = (values_in * norm_gain[0][None, :]).astype(jnp.bfloat16)
    query_sums = jnp.dot(scaled, query_weight[0], preferred_element_type=jnp.float32)
    pair_sums = jnp.dot(scaled, key_value_weight[0], preferred_element_type=jnp.float32)
    token_count = arrived.shape[0]
    own_rows = token_count // lax.axis_size("tensor")
    first_row = lax.axis_index("tensor") * own_rows
    query_sums, pair_sums, squares = (
        lax.psum(query_sums.astype(jnp.bfloat16), "tensor").astype(jnp.float32),
        lax.psum(pair_sums.astype(jnp.bfloat16), "tensor").astype(jnp.float32),
        lax.psum(squares.astype(jnp.bfloat16), "tensor").astype(jnp.float32),
    )
    query_local = lax.dynamic_slice_in_dim(query_sums, first_row, own_rows, 0)
    inverse = lax.rsqrt(squares / D + EPSILON)[:, None]
    positions = jnp.arange(token_count, dtype=jnp.int32)
    own_positions = first_row + jnp.arange(own_rows, dtype=jnp.int32)
    inverse_own = lax.dynamic_slice_in_dim(inverse, first_row, own_rows, 0)
    query_part = query_local * inverse_own
    queries = rotate(query_part.reshape(own_rows, -1, HD), own_positions).astype(jnp.bfloat16)
    pair_rows = (pair_sums * inverse).reshape(token_count, -1, 2, HD)
    key_rows = rotate(pair_rows[:, :, 0], positions).astype(jnp.bfloat16)
    value_rows = pair_rows[:, :, 1].astype(jnp.bfloat16)
    group_count = key_rows.shape[1]
    grouped = queries.reshape(own_rows, group_count, -1, HD)
    scores = jnp.einsum(
        "qgrd,kgd->grqk", grouped, key_rows, preferred_element_type=jnp.float32
    ) * HD ** (-0.5)
    causal = positions[None, :] <= own_positions[:, None]
    scores = jnp.where(causal[None, None], scores, -1e30)
    maximum = jnp.max(scores, axis=-1, keepdims=True)
    weights = jnp.exp(scores - maximum)
    probabilities = (weights / jnp.sum(weights, axis=-1, keepdims=True)).astype(jnp.bfloat16)
    attended = jnp.einsum(
        "grqk,kgd->qgrd", probabilities, value_rows, preferred_element_type=jnp.float32
    ).astype(jnp.bfloat16)
    return attended.reshape(own_rows, -1)[None]


def solution(mesh):
    placed = (
        P("section", "tensor", "dp"),
        P("section", "dp", "tensor"),
        P("section", "dp", "tensor"),
        P("section", "tensor"),
        P("section", "tensor", "dp"),
        P("section", "tensor", "dp"),
    )
    return jax.shard_map(
        per_device,
        mesh=mesh,
        in_specs=placed,
        out_specs=P("section", "tensor", "dp"),
        check_vma=False,
    )
```

profile of v0, /device:TPU:2, one launch (start us, length us, event | category | flops | bytes accessed | tf_op | source)
XLA Modules:
  0.0 486.2 jit_solution(7943351588400073942)
XLA Ops:
  6.5 0.7 all-gather.6.cloned.1.call-update
  7.3 108.6 %all-gather.6.cloned.1.call-done = bf16[1,1024,3584]{2,1,0:T(8,128)(2,1)} async-done(((bf16[1,64,3584]{2,1,0:T(8,128)(2,1)}), bf16[1,1024,3584]{2,1,0:T(8,128)(2,1)}) %all-gather.6.cloned.1.call-update) | async-done | bytes 7340048 | tf_op jit(solution)/shard_map/all_gather | solution.py:35
  115.9 9.1 %fusion.5 = bf16[1024,512]{1,0:T(8,128)(2,1)} fusion(bf16[1,3584,512]{2,1,0:T(8,128)(2,1)} %param.7, bf16[1,1024,3584]{2,1,0:T(8,128)(2,1)} %all-gather.6.cloned.1.call-done), kind=kOutput, calls=%fused_computation.7 | convolution fusion | flops 3758620672 | bytes 12058624 | tf_op jit(solution)/shard_map/dot_general | solution.py:34
  125.0 33.0 %reduce-scatter.2.cloned.1.call-done = bf16[128,512]{1,0:T(8,128)(2,1)} async-done(((bf16[1024,512]{1,0:T(8,128)(2,1)}), bf16[128,512]{1,0:T(8,128)(2,1)}) %reduce-scatter.2.cloned.1.call-update) | async-done | bytes 131088 | tf_op jit(solution)/shard_map/reduce_scatter | solution.py:39
  158.0 1.6 fusion.30
  159.7 32.3 %all-gather.4.cloned.1.call-done = bf16[1024,512]{1,0:T(8,128)(2,1)} async-done(((bf16[128,512]{1,0:T(8,128)(2,1)}), bf16[1024,512]{1,0:T(8,128)(2,1)}) %all-gather.4.cloned.1.call-update) | async-done | bytes 1048592 | tf_op jit(solution)/shard_map/all_gather | solution.py:43
  192.0 7.2 %collective-permute-start = (bf16[1024,512]{1,0:T(8,128)(2,1)}, bf16[1024,512]{1,0:T(8,128)(2,1)S(1)}, u32[]{:S(2)}, u32[]{:S(2)}) collective-permute-start(bf16[1024,512]{1,0:T(8,128)(2,1)} %all-gather.4.cloned.1.call-done), channel_id=1, source_target_pairs={{0,128},{128,256},{256,384},{384,0},{1,129},{129,257},{257,385},{3... | collective-permute-start | bytes 3145736 | tf_op jit(solution)/shard_map/ppermute | solution.py:15
  199.2 55.4 %collective-permute-done = bf16[1024,512]{1,0:T(8,128)(2,1)S(1)} collective-permute-done((bf16[1024,512]{1,0:T(8,128)(2,1)}, bf16[1024,512]{1,0:T(8,128)(2,1)S(1)}, u32[]{:S(2)}, u32[]{:S(2)}) %collective-permute-start) | collective-permute-done | bytes 1048608 | tf_op jit(solution)/shard_map/ppermute | solution.py:15
  254.6 1.3 convolution_convert_fusion.1
  255.8 1.8 convolution_convert_fusion
  257.8 0.2 multiply_cosine_fusion.1
  258.0 0.3 fusion.4
  258.2 79.6 %psum.22 = bf16[1024]{0:T(1024)(128)(2,1)S(1)} all-reduce(bf16[1024]{0:T(1024)(128)(2,1)S(1)} %fusion.4), channel_id=1, replica_groups=mesh['section'=4,'dp'=8,'tensor'=16] {'tensor'}, use_global_device_ids=true, to_apply=%region_3.0 | all-reduce | flops 1024 | bytes 4096 | tf_op jit(solution)/shard_map/psum | solution.py:56
  337.9 133.5 %all-reduce.3.cloned.1.call-done = (bf16[1024,256]{1,0:T(8,128)(2,1)}, bf16[1024,512]{1,0:T(8,128)(2,1)}) async-done(((bf16[1024,256]{1,0:T(8,128)(2,1)}, bf16[1024,512]{1,0:T(8,128)(2,1)}), (bf16[1024,256]{1,0:T(8,128)(2,1)}, bf16[1024,512]{1,0:T(8,128)(2,1)})) %all-reduce.3.cloned.1.call-update) | async-done | bytes 1572880 | tf_op jit(solution)/shard_map/psum | solution.py:55
  471.5 1.2 convert_multiply_fusion.2
  472.7 0.5 reshape.223
  473.3 0.4 slice.26
  473.6 0.5 slice.25
  474.2 0.9 convert_multiply_fusion.3
  475.3 2.4 fusion.33
  477.8 0.5 fusion.40
  478.3 0.3 fusion.13
  478.6 0.4 fusion.12
  479.1 0.7 broadcast_in_dim_reshape.3
  (26 shorter events, 0.7 us)
Async XLA Ops:
  6.5 249.3 %copy-start = (bf16[1,512,512]{2,1,0:T(8,128)(2,1)S(1)}, bf16[1,512,512]{2,1,0:T(8,128)(2,1)}, u32[]{:S(2)}) copy-start(bf16[1,512,512]{2,1,0:T(8,128)(2,1)} %param.10) | copy-start | bytes 1572868
  6.5 109.4 %all-gather.6.cloned.1.call-start = ((), (), s32[]{:S(2)}) async-start(), calls=%async_computation.3 | async-start | bytes 7798784 | tf_op jit(solution)/shard_map/all_gather | solution.py:35
  7.3 150.7 %copy-start.1 = (bf16[1,128,512]{2,1,0:T(8,128)(2,1)S(1)}, bf16[1,128,512]{2,1,0:T(8,128)(2,1)}, u32[]{:S(2)}) copy-start(bf16[1,128,512]{2,1,0:T(8,128)(2,1)} %param.8) | copy-start | bytes 393220
  7.3 247.3 %copy-start.2 = (bf16[1,512,256]{2,1,0:T(8,128)(2,1)S(1)}, bf16[1,512,256]{2,1,0:T(8,128)(2,1)}, u32[]{:S(2)}) copy-start(bf16[1,512,256]{2,1,0:T(8,128)(2,1)} %param.11) | copy-start | bytes 786436
  7.3 247.3 %copy-start.3 = (f32[1,512]{1,0:T(1,128)S(1)}, f32[1,512]{1,0:T(1,128)}, u32[]{:S(2)}) copy-start(f32[1,512]{1,0:T(1,128)} %param.9) | copy-start | bytes 6148
  7.3 150.7 %reduce-scatter.2.cloned.1.call-start = ((), (), s32[]{:S(2)}) async-start(), calls=%async_computation.1 | async-start | bytes 1179648 | tf_op jit(solution)/shard_map/reduce_scatter | solution.py:39
  125.0 67.0 %all-gather.4.cloned.1.call-start = ((), (), s32[]{:S(2)}) async-start(), calls=%async_computation.2 | async-start | bytes 1179648 | tf_op jit(solution)/shard_map/all_gather | solution.py:43
  159.6 311.9 %all-reduce.3.cloned.1.call-start = ((), (), s32[]{:S(2)}) async-start(), calls=%async_computation.4 | async-start | bytes 3145728 | tf_op jit(solution)/shard_map/psum | solution.py:55
  192.0 62.6 %collective-permute-start = (bf16[1024,512]{1,0:T(8,128)(2,1)}, bf16[1024,512]{1,0:T(8,128)(2,1)S(1)}, u32[]{:S(2)}, u32[]{:S(2)}) collective-permute-start(bf16[1024,512]{1,0:T(8,128)(2,1)} %all-gather.4.cloned.1.call-done), channel_id=1, source_target_pairs={{0,128},{128,256},{256,384},{384,0},{1,129},{129,257},{257,385},{3... | collective-permute-start | bytes 3145736 | tf_op jit(solution)/shard_map/ppermute | solution.py:15
Sparse Core Ops, SparseCore 0:
  9.4 106.4 all-gather.5
  125.1 32.8 reduce-scatter.1
  160.1 31.7 all-gather.3
  257.7 213.6 all-reduce.2
where the time goes:
time: 486 us
  waiting for transfers between devices  364 us (75%)
  blocking collectives  79.6 us (16%)
  between operations  13.3 us (3%)
  matrix products  12.9 us (3%)
  starting transfers between devices  7.32 us (2%)
  other arithmetic  7.13 us (1%)
    psum x1, waiting for transfers between devices, per_device(): lax.psum(pair_sums.astype(jnp.bfloat16), 'tensor').astype(jnp.float32)  134 us
    all_gather x1, waiting for transfers between devices, per_device(): lax.all_gather(hidden[0], 'tensor', axis=0, tiled=True)  109 us
    psum x1, blocking collectives, per_device(): lax.psum(squares.astype(jnp.bfloat16), 'tensor').astype(jnp.float32)  79.6 us
    ppermute x1, waiting for transfers between devices, passed_along(): return lax.ppermute(value, axis, pairs)  55.4 us
    reduce_scatter x1, waiting for transfers between devices, per_device(): lax.psum_scatter(partials.astype(jnp.bfloat16), 'dp', scatter_dimension=0...  33 us
    all_gather x1, waiting for transfers between devices, per_device(): gathered = lax.all_gather(boundary, 'dp', axis=0, tiled=True)  32.3 us
  transfers between devices with their start and end apart: 5, of which 5 were waited for; matrix products, arithmetic and copies ran while one was open for 0% of the time, Pallas kernels for 0%

commit v1 on v0

--- a/solution.py
+++ b/solution.py
@@ -40,7 +40,12 @@
         partials.astype(jnp.bfloat16), "dp", scatter_dimension=0, tiled=True
     ).astype(jnp.float32)
     boundary = (residual[0].astype(jnp.float32) + summed).astype(jnp.bfloat16)
-    gathered = lax.all_gather(boundary, "dp", axis=0, tiled=True)
+    ring = [boundary]
+    for hop in range(7):
+        ring.append(lax.ppermute(ring[-1], "dp", [(dev, (dev + 1) % 8) for dev in range(8)]))
+    gathered = jnp.roll(
+        jnp.concatenate(ring[::-1], axis=0), (lax.axis_index("dp") + 1) * ring[0].shape[0], axis=0
+    )
     arrived = passed_along(gathered, "section", 1)
     values_in = arrived.astype(jnp.float32)
     squares = jnp.sum(values_in * values_in, axis=1)

time: 486 us -> 489 us (level)
    ppermute x0 -> x7, waiting for transfers between devices: none -> 35.2 us  [per_device(): lax.ppermute(ring[-1], 'dp', [(dev, (dev + 1) % 8) for dev in range(8)])]
    all_gather x1 -> x0, waiting for transfers between devices: 32.3 us -> none  [per_device(): gathered = lax.all_gather(boundary, 'dp', axis=0, tiled=True)]
  transfers between devices with their start and end apart: 5 -> 11, of which waited for: 5 -> 11; matrix products, arithmetic and copies ran while one was open for 0% -> 0% of each run, Pallas kernels for 0% -> 0%
where the time goes in v1:
time: 489 us
  waiting for transfers between devices  366 us (75%)
  blocking collectives  79.6 us (16%)
  between operations  13.4 us (3%)
  matrix products  12.9 us (3%)
  starting transfers between devices  7.94 us (2%)
  other arithmetic  6.48 us (1%)
    psum x1, waiting for transfers between devices, per_device(): lax.psum(pair_sums.astype(jnp.bfloat16), 'tensor').astype(jnp.float32)  138 us
    all_gather x1, waiting for transfers between devices, per_device(): lax.all_gather(hidden[0], 'tensor', axis=0, tiled=True)  109 us
    psum x1, blocking collectives, per_device(): lax.psum(squares.astype(jnp.bfloat16), 'tensor').astype(jnp.float32)  79.6 us
    ppermute x1, waiting for transfers between devices, passed_along(): return lax.ppermute(value, axis, pairs)  50.6 us
    ppermute x7, waiting for transfers between devices, per_device(): lax.ppermute(ring[-1], 'dp', [(dev, (dev + 1) % 8) for dev in range(8)])  35.2 us
    reduce_scatter x1, waiting for transfers between devices, per_device(): lax.psum_scatter(partials.astype(jnp.bfloat16), 'dp', scatter_dimension=0...  33 us
  transfers between devices with their start and end apart: 11, of which 11 were waited for; matrix products, arithmetic and copies ran while one was open for 0% of the time, Pallas kernels for 0%

profile of v1, /device:TPU:2, one launch (start us, length us, event | category | flops | bytes accessed | tf_op | source)
XLA Modules:
  0.0 489.1 jit_solution(20431677967576334)
XLA Ops:
  6.5 0.7 all-gather.3.cloned.1.call-update
  7.3 108.6 %all-gather.3.cloned.1.call-done = bf16[1,1024,3584]{2,1,0:T(8,128)(2,1)} async-done(((bf16[1,64,3584]{2,1,0:T(8,128)(2,1)}), bf16[1,1024,3584]{2,1,0:T(8,128)(2,1)}) %all-gather.3.cloned.1.call-update) | async-done | bytes 7340048 | tf_op jit(solution)/shard_map/all_gather | solution.py:35
  115.9 9.1 %fusion.5 = bf16[1024,512]{1,0:T(8,128)(2,1)} fusion(bf16[1,3584,512]{2,1,0:T(8,128)(2,1)} %param.7, bf16[1,1024,3584]{2,1,0:T(8,128)(2,1)} %all-gather.3.cloned.1.call-done), kind=kOutput, calls=%fused_computation.7 | convolution fusion | flops 3758620672 | bytes 12058624 | tf_op jit(solution)/shard_map/dot_general | solution.py:34
  125.1 33.0 %reduce-scatter.2.cloned.1.call-done = bf16[128,512]{1,0:T(8,128)(2,1)} async-done(((bf16[1024,512]{1,0:T(8,128)(2,1)}), bf16[128,512]{1,0:T(8,128)(2,1)}) %reduce-scatter.2.cloned.1.call-update) | async-done | bytes 131088 | tf_op jit(solution)/shard_map/reduce_scatter | solution.py:39
  158.0 0.9 fusion.30
  159.0 4.4 collective-permute-done
  163.4 4.4 collective-permute-done.1
  167.7 4.4 collective-permute-done.2
  172.1 5.3 %collective-permute-done.3 = bf16[128,512]{1,0:T(8,128)(2,1)S(1)} collective-permute-done((bf16[128,512]{1,0:T(8,128)(2,1)S(1)}, bf16[128,512]{1,0:T(8,128)(2,1)S(1)}, u32[]{:S(2)}, u32[]{:S(2)}) %collective-permute-start.3) | collective-permute-done | bytes 131104 | tf_op jit(solution)/shard_map/ppermute | solution.py:45
  177.4 5.6 %collective-permute-done.4 = bf16[128,512]{1,0:T(8,128)(2,1)S(1)} collective-permute-done((bf16[128,512]{1,0:T(8,128)(2,1)S(1)}, bf16[128,512]{1,0:T(8,128)(2,1)S(1)}, u32[]{:S(2)}, u32[]{:S(2)}) %collective-permute-start.4) | collective-permute-done | bytes 131104 | tf_op jit(solution)/shard_map/ppermute | solution.py:45
  183.0 5.6 %collective-permute-done.5 = bf16[128,512]{1,0:T(8,128)(2,1)S(1)} collective-permute-done((bf16[128,512]{1,0:T(8,128)(2,1)S(1)}, bf16[128,512]{1,0:T(8,128)(2,1)S(1)}, u32[]{:S(2)}, u32[]{:S(2)}) %collective-permute-start.5) | collective-permute-done | bytes 131104 | tf_op jit(solution)/shard_map/ppermute | solution.py:45
  188.6 5.6 %collective-permute-done.6 = bf16[128,512]{1,0:T(8,128)(2,1)S(1)} collective-permute-done((bf16[128,512]{1,0:T(8,128)(2,1)S(1)}, bf16[128,512]{1,0:T(8,128)(2,1)S(1)}, u32[]{:S(2)}, u32[]{:S(2)}) %collective-permute-start.6) | collective-permute-done | bytes 131104 | tf_op jit(solution)/shard_map/ppermute | solution.py:45
  194.6 7.8 %collective-permute-start.7 = (bf16[1024,512]{1,0:T(8,128)(2,1)S(1)}, bf16[1024,512]{1,0:T(8,128)(2,1)S(1)}, u32[]{:S(2)}, u32[]{:S(2)}) collective-permute-start(bf16[1024,512]{1,0:T(8,128)(2,1)S(1)} %constant_dynamic-slice_fusion), channel_id=1, source_target_pairs={{0,128},{128,256},{256,384},{384,0},{1,129},{129,257},{257,385},{3... | collective-permute-start | bytes 3145736 | tf_op jit(solution)/shard_map/ppermute | solution.py:15
  202.5 50.6 %collective-permute-done.7 = bf16[1024,512]{1,0:T(8,128)(2,1)S(1)} collective-permute-done((bf16[1024,512]{1,0:T(8,128)(2,1)S(1)}, bf16[1024,512]{1,0:T(8,128)(2,1)S(1)}, u32[]{:S(2)}, u32[]{:S(2)}) %collective-permute-start.7) | collective-permute-done | bytes 1048608 | tf_op jit(solution)/shard_map/ppermute | solution.py:15
  253.1 1.7 convolution_convert_fusion
  254.8 1.3 convolution_convert_fusion.1
  256.7 79.6 %psum.22 = bf16[1024]{0:T(1024)(128)(2,1)S(1)} all-reduce(bf16[1024]{0:T(1024)(128)(2,1)S(1)} %fusion.4), channel_id=1, replica_groups=mesh['section'=4,'dp'=8,'tensor'=16] {'tensor'}, use_global_device_ids=true, to_apply=%region_3.4 | all-reduce | flops 1024 | bytes 4096 | tf_op jit(solution)/shard_map/psum | solution.py:61
  336.4 138.0 %all-reduce.3.cloned.1.call-done = (bf16[1024,256]{1,0:T(8,128)(2,1)}, bf16[1024,512]{1,0:T(8,128)(2,1)}) async-done(((bf16[1024,256]{1,0:T(8,128)(2,1)}, bf16[1024,512]{1,0:T(8,128)(2,1)}), (bf16[1024,256]{1,0:T(8,128)(2,1)}, bf16[1024,512]{1,0:T(8,128)(2,1)})) %all-reduce.3.cloned.1.call-update) | async-done | bytes 1572880 | tf_op jit(solution)/shard_map/psum | solution.py:60
  474.4 1.2 convert_multiply_fusion.2
  475.6 0.5 reshape.223
  476.5 0.5 slice.25
  477.1 0.9 convert_multiply_fusion.3
  478.2 2.4 fusion.33
  482.0 0.7 broadcast_in_dim_reshape.3
  (54 shorter events, 2.9 us)
Async XLA Ops:
  6.5 246.6 %copy-start = (bf16[1,512,512]{2,1,0:T(8,128)(2,1)S(1)}, bf16[1,512,512]{2,1,0:T(8,128)(2,1)}, u32[]{:S(2)}) copy-start(bf16[1,512,512]{2,1,0:T(8,128)(2,1)} %param.10) | copy-start | bytes 1572868
  6.5 109.4 %all-gather.3.cloned.1.call-start = ((), (), s32[]{:S(2)}) async-start(), calls=%async_computation.2 | async-start | bytes 7798784 | tf_op jit(solution)/shard_map/all_gather | solution.py:35
  7.3 150.7 %copy-start.1 = (bf16[1,128,512]{2,1,0:T(8,128)(2,1)S(1)}, bf16[1,128,512]{2,1,0:T(8,128)(2,1)}, u32[]{:S(2)}) copy-start(bf16[1,128,512]{2,1,0:T(8,128)(2,1)} %param.8) | copy-start | bytes 393220
  7.3 150.7 %reduce-scatter.2.cloned.1.call-start = ((), (), s32[]{:S(2)}) async-start(), calls=%async_computation.1 | async-start | bytes 1179648 | tf_op jit(solution)/shard_map/reduce_scatter | solution.py:39
  125.0 349.4 %all-reduce.3.cloned.1.call-start = ((), (), s32[]{:S(2)}) async-start(), calls=%async_computation.3 | async-start | bytes 3145728 | tf_op jit(solution)/shard_map/psum | solution.py:60
  158.9 4.4 collective-permute-start
  163.4 4.4 collective-permute-start.1
  167.7 4.4 collective-permute-start.2
  172.1 5.3 %collective-permute-start.3 = (bf16[128,512]{1,0:T(8,128)(2,1)S(1)}, bf16[128,512]{1,0:T(8,128)(2,1)S(1)}, u32[]{:S(2)}, u32[]{:S(2)}) collective-permute-start(bf16[128,512]{1,0:T(8,128)(2,1)S(1)} %collective-permute-done.2), channel_id=1, source_target_pairs={{0,16},{16,32},{32,48},{48,64},{64,80},{80,96},{96,112},{112,0},{1... | collective-permute-start | bytes 393224 | tf_op jit(solution)/shard_map/ppermute | solution.py:45
  177.4 5.6 %collective-permute-start.4 = (bf16[128,512]{1,0:T(8,128)(2,1)S(1)}, bf16[128,512]{1,0:T(8,128)(2,1)S(1)}, u32[]{:S(2)}, u32[]{:S(2)}) collective-permute-start(bf16[128,512]{1,0:T(8,128)(2,1)S(1)} %collective-permute-done.3), channel_id=1, source_target_pairs={{0,16},{16,32},{32,48},{48,64},{64,80},{80,96},{96,112},{112,0},{1... | collective-permute-start | bytes 393224 | tf_op jit(solution)/shard_map/ppermute | solution.py:45
  183.0 5.6 %collective-permute-start.5 = (bf16[128,512]{1,0:T(8,128)(2,1)S(1)}, bf16[128,512]{1,0:T(8,128)(2,1)S(1)}, u32[]{:S(2)}, u32[]{:S(2)}) collective-permute-start(bf16[128,512]{1,0:T(8,128)(2,1)S(1)} %collective-permute-done.4), channel_id=1, source_target_pairs={{0,16},{16,32},{32,48},{48,64},{64,80},{80,96},{96,112},{112,0},{1... | collective-permute-start | bytes 393224 | tf_op jit(solution)/shard_map/ppermute | solution.py:45
  188.6 5.6 %collective-permute-start.6 = (bf16[128,512]{1,0:T(8,128)(2,1)S(1)}, bf16[128,512]{1,0:T(8,128)(2,1)S(1)}, u32[]{:S(2)}, u32[]{:S(2)}) collective-permute-start(bf16[128,512]{1,0:T(8,128)(2,1)S(1)} %collective-permute-done.5), channel_id=1, source_target_pairs={{0,16},{16,32},{32,48},{48,64},{64,80},{80,96},{96,112},{112,0},{1... | collective-permute-start | bytes 393224 | tf_op jit(solution)/shard_map/ppermute | solution.py:45
  194.4 58.7 %copy-start.3 = (f32[1,512]{1,0:T(1,128)S(1)}, f32[1,512]{1,0:T(1,128)}, u32[]{:S(2)}) copy-start(f32[1,512]{1,0:T(1,128)} %param.9) | copy-start | bytes 6148
  194.6 60.2 %copy-start.2 = (bf16[1,512,256]{2,1,0:T(8,128)(2,1)S(1)}, bf16[1,512,256]{2,1,0:T(8,128)(2,1)}, u32[]{:S(2)}) copy-start(bf16[1,512,256]{2,1,0:T(8,128)(2,1)} %param.11) | copy-start | bytes 786436
  194.6 58.5 %collective-permute-start.7 = (bf16[1024,512]{1,0:T(8,128)(2,1)S(1)}, bf16[1024,512]{1,0:T(8,128)(2,1)S(1)}, u32[]{:S(2)}, u32[]{:S(2)}) collective-permute-start(bf16[1024,512]{1,0:T(8,128)(2,1)S(1)} %constant_dynamic-slice_fusion), channel_id=1, source_target_pairs={{0,128},{128,256},{256,384},{384,0},{1,129},{129,257},{257,385},{3... | collective-permute-start | bytes 3145736 | tf_op jit(solution)/shard_map/ppermute | solution.py:15
Sparse Core Ops, SparseCore 0:
  9.4 106.4 all-gather.2
  125.1 32.8 reduce-scatter.1
  256.2 218.1 all-reduce.2
